TPU v7x, 32 devices: a whole 2x2x4 slice. The times are simulated.
32 devices in a mesh: fsdp: 16 (over z, x, core), rep: 2 (over y).
Axes of the slice: x: 2, y: 2, z: 4, core: 2. Of those that a mesh axis runs over, the one named last changes fastest.
Arguments:
- layer_input: bfloat16 [128, 256, 768], P(('fsdp', 'rep')), may hold values from -6 to 6
- slot_valid: int32 [128, 256], P(('fsdp', 'rep')), may hold values from 0 to 1, as said below
- projections: bfloat16 [3, 768, 768], P(None, 'fsdp'), may hold values from -0.21875 to 0.21875
- out_weight: bfloat16 [768, 768], P('fsdp'), may hold values from -1.25 to 1.25
- vectors: bfloat16 [8, 768], P(None, 'fsdp'), may hold values from -2 to 2
- up_weight: bfloat16 [768, 3072], P('fsdp'), may hold values from -0.21875 to 0.21875
- up_bias: bfloat16 [3072], P('fsdp'), may hold values from -3 to 3
- down_weight: bfloat16 [3072, 768], P('fsdp'), may hold values from -0.109375 to 0.109375
- cotangent: bfloat16 [128, 256, 768], P(('fsdp', 'rep')), may hold values from -6 to 6
Outputs:
- output: bfloat16 [128, 256, 768], P(('fsdp', 'rep'))
- grad_input: bfloat16 [128, 256, 768], P(('fsdp', 'rep'))
- grad_projections: float32 [3, 768, 768], P(None, 'fsdp')
- grad_out_weight: float32 [768, 768], P('fsdp')
- grad_vectors: float32 [8, 768], P(None, 'fsdp')
- grad_up_weight: float32 [768, 3072], P('fsdp')
- grad_up_bias: float32 [3072], P('fsdp')
- grad_down_weight: float32 [3072, 768], P('fsdp')
Inputs may be any that keep to these rules, and one draw needn't show every extreme that they name: `slot_valid`: in each sequence the first 128 slots are 1; of the next 128 slots the first k are 1 and the rest 0, with k from 10 to 100, both of which occur in every draw.
All inputs are finite; a program needn't handle non-finite values.
Results may differ from a plain program's by a relative error of at most 0.02.
Values may be sent and summed in bfloat16 or wider, within the bound.
No kernel may reach another device: no remote copies, remote signals or barrier semaphores. Data moves between devices by JAX's collectives and lax.ppermute only.
A program may use at most 192 MiB of HBM per device.

v0:
```python
from functools import partial
import jax
import jax.numpy as jnp
from jax import lax
from jax.sharding import PartitionSpec as P

HEADS = 12
HD = 64
EPSILON = 1e-12
MASKED = -1e30


def normalize(values, gain, shift):
    centered = values - jnp.mean(values, axis=-1, keepdims=True)
    spread = jnp.mean(centered * centered, axis=-1, keepdims=True)
    return centered * lax.rsqrt(spread + EPSILON) * gain + shift


def column_sum(values):
    return jnp.sum(values.astype(jnp.float32), axis=0)


def body(
    layer_input,
    slot_valid,
    projections,
    out_weight,
    vectors,
    up_weight,
    up_bias,
    down_weight,
    cotangent,
):
    seq_count, slot_count, model_width = layer_input.shape
    score_scale = HD ** (-0.5)
    shape_heads = (seq_count, slot_count, HEADS, HD)
    qkv_all, out_all, vec_all = (
        lax.all_gather(projections, "fsdp", axis=1, tiled=True),
        lax.all_gather(out_weight, "fsdp", axis=0, tiled=True),
        lax.all_gather(vectors, "fsdp", axis=1, tiled=True),
    )
    in_all, bias_in_all, down_all = (
        lax.all_gather(up_weight, "fsdp", axis=0, tiled=True),
        lax.all_gather(up_bias, "fsdp", axis=0, tiled=True),
        lax.all_gather(down_weight, "fsdp", axis=0, tiled=True),
    )
    bias_q, bias_v, bias_out, gain_one, shift_one, bias_down, gain_two, shift_two = vec_all.astype(
        jnp.float32
    )
    token_rows = layer_input.reshape(-1, model_width)
    query_low = (
        jnp.dot(token_rows, qkv_all[0], preferred_element_type=jnp.float32) + bias_q
    ).astype(jnp.bfloat16)
    key_low = jnp.dot(token_rows, qkv_all[1], preferred_element_type=jnp.float32).astype(
        jnp.bfloat16
    )
    value_low = (
        jnp.dot(token_rows, qkv_all[2], preferred_element_type=jnp.float32) + bias_v
    ).astype(jnp.bfloat16)
    query_heads = query_low.reshape(shape_heads)
    key_heads = key_low.reshape(shape_heads)
    value_heads = value_low.reshape(shape_heads)
    key_live = (slot_valid > 0)[:, None, None, :]

    def scores_of():
        raw = (
            jnp.einsum(
                "nqhe,nkhe->nhqk", query_heads, key_heads, preferred_element_type=jnp.float32
            )
            * score_scale
        )
        return jnp.where(key_live, raw, MASKED)

    scores = scores_of()
    row_max = jnp.max(scores, axis=-1, keepdims=True)
    exp_scores = jnp.exp(scores - row_max)
    exp_total = jnp.sum(exp_scores, axis=-1, keepdims=True)
    log_total = row_max + jnp.log(exp_total)
    probs_low = (exp_scores / exp_total).astype(jnp.bfloat16)
    context = jnp.einsum(
        "nhqk,nkhe->nqhe", probs_low, value_heads, preferred_element_type=jnp.float32
    )
    context = context.reshape(-1, model_width).astype(jnp.bfloat16)
    first_sum = (
        token_rows.astype(jnp.float32)
        + jnp.dot(context, out_all, preferred_element_type=jnp.float32)
        + bias_out
    )
    normed, norm_one_back = jax.vjp(normalize, first_sum, gain_one, shift_one)
    normed_low = normed.astype(jnp.bfloat16)
    hidden_pre = jnp.dot(
        normed_low, in_all, preferred_element_type=jnp.float32
    ) + bias_in_all.astype(jnp.float32)
    activated, gelu_back = jax.vjp(partial(jax.nn.gelu, approximate=False), hidden_pre)
    active_low = activated.astype(jnp.bfloat16)
    second_sum = (
        normed + jnp.dot(active_low, down_all, preferred_element_type=jnp.float32) + bias_down
    )
    normed_two, norm_two_back = jax.vjp(normalize, second_sum, gain_two, shift_two)
    row_live = slot_valid.reshape(-1, 1).astype(jnp.float32)
    output = (normed_two * row_live).astype(jnp.bfloat16).reshape(layer_input.shape)
    grad_rows = cotangent.reshape(-1, model_width).astype(jnp.float32) * row_live
    grad_second, grad_gain_two, grad_shift_two = norm_two_back(grad_rows)
    grad_second_low = grad_second.astype(jnp.bfloat16)
    in_back, down_back = (
        lax.all_gather(up_weight, "fsdp", axis=0, tiled=True),
        lax.all_gather(down_weight, "fsdp", axis=0, tiled=True),
    )
    grad_down = jnp.dot(active_low.T, grad_second_low, preferred_element_type=jnp.float32)
    grad_bias_down = column_sum(grad_second_low)
    grad_active = jnp.dot(grad_second_low, down_back.T, preferred_element_type=jnp.float32)
    grad_hidden_low = gelu_back(grad_active)[0].astype(jnp.bfloat16)
    grad_up = jnp.dot(normed_low.T, grad_hidden_low, preferred_element_type=jnp.float32)
    grad_bias_up = column_sum(grad_hidden_low)
    grad_normed = grad_second_low.astype(jnp.float32) + jnp.dot(
        grad_hidden_low, in_back.T, preferred_element_type=jnp.float32
    )
    ffn_parts = (
        lax.psum_scatter(
            grad_up.astype(jnp.bfloat16), "fsdp", scatter_dimension=0, tiled=True
        ).astype(jnp.float32),
        lax.psum_scatter(
            grad_bias_up.astype(jnp.bfloat16), "fsdp", scatter_dimension=0, tiled=True
        ).astype(jnp.float32),
        lax.psum_scatter(
            grad_down.astype(jnp.bfloat16), "fsdp", scatter_dimension=0, tiled=True
        ).astype(jnp.float32),
    )
    ffn_parts = (
        lax.psum(ffn_parts[0].astype(jnp.bfloat16), "rep").astype(jnp.float32),
        lax.psum(ffn_parts[1].astype(jnp.bfloat16), "rep").astype(jnp.float32),
        lax.psum(ffn_parts[2].astype(jnp.bfloat16), "rep").astype(jnp.float32),
    )
    grad_first, grad_gain_one, grad_shift_one = norm_one_back(grad_normed)
    grad_first_low = grad_first.astype(jnp.bfloat16)
    qkv_back, out_back = (
        lax.all_gather(projections, "fsdp", axis=1, tiled=True),
        lax.all_gather(out_weight, "fsdp", axis=0, tiled=True),
    )
    grad_out = jnp.dot(context.T, grad_first_low, preferred_element_type=jnp.float32)
    grad_bias_out = column_sum(grad_first_low)
    grad_context = (
        jnp.dot(grad_first_low, out_back.T, preferred_element_type=jnp.float32)
        .astype(jnp.bfloat16)
        .reshape(shape_heads)
    )
    weights_soft = jnp.exp(scores_of() - log_total)
    probs_again = weights_soft.astype(jnp.bfloat16)
    grad_value = jnp.einsum(
        "nhqk,nqhe->nkhe", probs_again, grad_context, preferred_element_type=jnp.float32
    )
    grad_value = grad_value.reshape(-1, model_width).astype(jnp.bfloat16)
    grad_probs = jnp.einsum(
        "nqhe,nkhe->nhqk", grad_context, value_heads, preferred_element_type=jnp.float32
    )
    grad_scores = (
        weights_soft * (grad_probs - jnp.sum(weights_soft * grad_probs, axis=-1, keepdims=True))
    ).astype(jnp.bfloat16)
    grad_query = (
        jnp.einsum("nhqk,nkhe->nqhe", grad_scores, key_heads, preferred_element_type=jnp.float32)
        * score_scale
    )
    grad_query = grad_query.reshape(-1, model_width).astype(jnp.bfloat16)
    grad_key = (
        jnp.einsum("nhqk,nqhe->nkhe", grad_scores, query_heads, preferred_element_type=jnp.float32)
        * score_scale
    )
    grad_key = grad_key.reshape(-1, model_width).astype(jnp.bfloat16)
    grad_stack = jnp.stack(
        [
            jnp.dot(token_rows.T, grad_query, preferred_element_type=jnp.float32),
            jnp.dot(token_rows.T, grad_key, preferred_element_type=jnp.float32),
            jnp.dot(token_rows.T, grad_value, preferred_element_type=jnp.float32),
        ]
    )
    grad_vectors = jnp.stack(
        [
            column_sum(grad_query),
            column_sum(grad_value),
            grad_bias_out,
            grad_gain_one,
            grad_shift_one,
            grad_bias_down,
            grad_gain_two,
            grad_shift_two,
        ]
    )
    grad_total = grad_first_low.astype(jnp.float32)
    grad_total = grad_total + jnp.dot(grad_query, qkv_back[0].T, preferred_element_type=jnp.float32)
    grad_total = grad_total + jnp.dot(grad_key, qkv_back[1].T, preferred_element_type=jnp.float32)
    grad_total = grad_total + jnp.dot(grad_value, qkv_back[2].T, preferred_element_type=jnp.float32)
    grad_input = grad_total.astype(jnp.bfloat16).reshape(layer_input.shape)
    attn_parts = (
        lax.psum_scatter(
            grad_stack.astype(jnp.bfloat16), "fsdp", scatter_dimension=1, tiled=True
        ).astype(jnp.float32),
        lax.psum_scatter(
            grad_out.astype(jnp.bfloat16), "fsdp", scatter_dimension=0, tiled=True
        ).astype(jnp.float32),
        lax.psum_scatter(
            grad_vectors.astype(jnp.bfloat16), "fsdp", scatter_dimension=1, tiled=True
        ).astype(jnp.float32),
    )
    attn_parts = (
        lax.psum(attn_parts[0].astype(jnp.bfloat16), "rep").astype(jnp.float32),
        lax.psum(attn_parts[1].astype(jnp.bfloat16), "rep").astype(jnp.float32),
        lax.psum(attn_parts[2].astype(jnp.bfloat16), "rep").astype(jnp.float32),
    )
    return (
        output,
        grad_input,
        attn_parts[0],
        attn_parts[1],
        attn_parts[2],
        ffn_parts[0],
        ffn_parts[1],
        ffn_parts[2],
    )


def solution(mesh):
    placed = (
        P(("fsdp", "rep"), None, None),
        P(("fsdp", "rep"), None),
        P(None, "fsdp", None),
        P("fsdp", None),
        P(None, "fsdp"),
        P("fsdp", None),
        P("fsdp"),
        P("fsdp", None),
        P(("fsdp", "rep"), None, None),
    )
    return jax.shard_map(
        body,
        mesh=mesh,
        in_specs=placed,
        out_specs=(
            P(("fsdp", "rep"), None, None),
            P(("fsdp", "rep"), None, None),
            P(None, "fsdp", None),
            P("fsdp", None),
            P(None, "fsdp"),
            P("fsdp", None),
            P("fsdp"),
            P("fsdp", None),
        ),
        check_vma=False,
    )
```

profile of v0, /device:TPU:0, one launch (start us, length us, event | category | flops | bytes accessed | tf_op | source)
XLA Modules:
  0.0 753.9 jit_solution(702271938507066873)
XLA Ops:
  10.7 1.3 fusion.54
  12.0 23.5 %all-gather = bf16[16,48,8]{1,2,0:T(8,128)(2,1)S(1)} all-gather(bf16[1,48,8]{1,2,0:T(8,128)(2,1)} %bitcast.138), channel_id=1, replica_groups=mesh['fsdp'=16,'rep'=2] {'fsdp'}, dimensions={0}, use_global_device_ids=true | all-gather | bytes 13056 | tf_op jit(solution)/shard_map/all_gather | solution.py:40
  35.6 1.3 fusion.55
  38.5 31.3 %all-reduce = bf16[3072]{0:T(1024)(128)(2,1)S(1)} all-reduce(bf16[3072]{0:T(1024)(128)(2,1)S(1)} %dynamic-update-slice), channel_id=1, replica_groups=mesh['fsdp'=16,'rep'=2] {'fsdp'}, use_global_device_ids=true, to_apply=%add | all-reduce | flops 3072 | bytes 12288
  69.8 3.2 convolution_convert_fusion.3
  73.8 1.2 reshape.153
  75.0 3.7 add_convert_fusion.4
  78.7 1.6 copy.54
  80.3 2.9 reshape.152
  83.2 4.8 add_convert_fusion.5
  88.1 2.6 copy.53
  90.6 3.9 reshape.151
  94.5 3.1 fusion.12
  97.6 3.8 fusion.6
  102.3 3.4 fusion.22
  105.7 1.2 copy.60
  107.0 1.5 copy.81
  108.5 4.0 fusion.56
  114.1 40.7 %all-gather.10.cloned.1.call-done = bf16[768,3072]{1,0:T(8,128)(2,1)} async-done(((bf16[48,3072]{1,0:T(8,128)(2,1)}), bf16[768,3072]{1,0:T(8,128)(2,1)}) %all-gather.10.cloned.1.call-update) | async-done | bytes 4718608 | tf_op jit(solution)/shard_map/all_gather | solution.py:43
  154.8 36.1 %multiply_convert_fusion.1 = (bf16[1024,3072]{1,0:T(8,128)(2,1)}, f32[1024,3072]{1,0:T(8,128)}, f32[1024,3072]{1,0:T(8,128)}) fusion(f32[3072]{0:T(1024)S(1)} %convert_element_type.182, bf16[768,3072]{1,0:T(8,128)(2,1)} %all-gather.10.cloned.1.call-done, f32[1024,768]{1,0:T(8,128)S(1)} %get-tuple-element.69, f32[768]{0:T(1024)S(1)} %get-tuple-element.40, ...), kind=kOutput, calls=%fused_computation.6 | convolution fusion | flops 5043388416 | bytes 39348224 | tf_op jit(solution)/shard_map/dot_general | solution.py:91
  190.9 17.7 %all-gather.12.cloned.1.call-done = bf16[3072,768]{1,0:T(8,128)(2,1)} async-done(((bf16[192,768]{1,0:T(8,128)(2,1)}), bf16[3072,768]{1,0:T(8,128)(2,1)}) %all-gather.12.cloned.1.call-update) | async-done | bytes 4718608 | tf_op jit(solution)/shard_map/all_gather | solution.py:45
  208.7 8.8 %fusion.57 = (f32[1024]{0:T(1024)S(1)}, f32[1024,768]{1,0:T(8,128)S(1)}) fusion(f32[768]{0:T(1024)S(1)} %get-tuple-element.39, bf16[1024,3072]{1,0:T(8,128)(2,1)} %get-tuple-element.59, bf16[3072,768]{1,0:T(8,128)(2,1)} %all-gather.12.cloned.1.call-done, f32[768]{0:T(1024)S(1)} %get-tuple-element.40, f32[768]{0:T(1024)S(1)} %get-tuple-element.41, ...), kind=kOutput, calls=%fused_computation.120 | convolution fusion | flops 4837342208 | bytes 17323008 | tf_op jit(solution)/shard_map/dot_general | solution.py:97
  218.9 1.5 multiply_reduce_fusion.2
  220.5 2.8 fusion.52
  223.7 17.3 %fusion.60 = (bf16[3072]{0:T(1024)(128)(2,1)S(1)}, bf16[1024,3072]{1,0:T(8,128)(2,1)}) fusion(f32[1024,3072]{1,0:T(8,128)} %get-tuple-element.60, bf16[1024,768]{1,0:T(8,128)(2,1)S(1)} %get-tuple-element.52, bf16[3072,768]{1,0:T(8,128)(2,1)} %all-gather.12.cloned.1.call-done, f32[1024,3072]{1,0:T(8,128)} %get-tuple-element.70, ...), kind=kOutput, calls=%fused_computation.123 | convolution fusion | flops 4882166784 | bytes 37767168 | tf_op jit(solution)/shard_map/dot_general | solution.py:111
  241.0 9.7 %multiply_reduce_fusion.3 = (bf16[768]{0:T(1024)(128)(2,1)S(1)}, f32[1024]{0:T(1024)S(1)}, bf16[768]{0:T(1024)(128)(2,1)S(1)}, f32[1024,768]{1,0:T(8,128)S(1)}) fusion(f32[1024,768]{1,0:T(8,128)S(1)} %copy-done.7, f32[1024]{0:T(1024)S(1)} %fusion.40, f32[1024]{0:T(1024)S(1)} %broadcast_multiply_fusion.1, f32[768]{0:T(1024)S(1)} %get-tuple-element.41, ...), kind=kOutput, calls=%fused_computation.37 | convolution fusion | flops 4839699456 | bytes 18892800 | tf_op jit(solution)/shard_map/dot_general | solution.py:115
  250.7 1.5 fusion.51
  253.7 2.6 convolution_convert_fusion.2
  256.2 2.7 copy.61
  258.9 3.9 reshape.155
  262.8 8.6 %multiply_reduce_fusion = (f32[4,12,256]{2,1,0:T(8,128)S(1)}, f32[4,12,256,256]{2,3,1,0:T(8,128)S(1)}) fusion(f32[4,12,256]{2,1,0:T(8,128)S(1)} %copy-done.20, f32[4,12,256,256]{2,3,1,0:T(8,128)} %copy-done, pred[4,256]{1,0:T(4,128)(4,1)S(1)} %copy-done.22, bf16[4,256,12,64]{1,0,3,2:T(4,128)(2,1)S(1)} %copy-done.9, bf16[4,256,12,64]{1,0,3,2:T(4,128)(2,1)} %reshape.155), kind=kOutput, calls=%fused_computation.3 | convolution fusion | flops 418369536 | bytes 28410880 | tf_op jit(solution)/shard_map/nqhe,nkhe->nhqk/dot_general | solution.py:153
  271.4 8.0 %multiply_convert_fusion = bf16[4,12,256,256]{2,3,1,0:T(8,128)(2,1)S(1)} fusion(f32[4,12,256,256]{2,3,1,0:T(8,128)S(1)} %get-tuple-element.75, f32[4,12,256]{2,1,0:T(8,128)S(1)} %get-tuple-element.74, f32[4,12,256]{2,1,0:T(8,128)S(1)} %copy-done.20, f32[4,12,256,256]{2,3,1,0:T(8,128)} %copy-done, pred[4,256]{1,0:T(4,128)(4,1)S(1)} %copy-done.22), kind=kLoop, calls=%fused_computation.2 | loop fusion | flops 18874368 | bytes 31556608 | tf_op jit(solution)/shard_map/convert_element_type | solution.py:158
  279.5 2.0 fusion.24
  281.6 1.3 fusion.58
  283.4 1.4 slice-done.2
  285.2 3.6 fusion.59
  288.8 1.2 copy.69
  290.5 1.2 copy.66
  292.1 1.2 copy.72
  294.0 1.4 fusion.27
  295.4 1.4 fusion.26
  296.9 1.4 fusion.25
  298.3 2.0 pad_maximum_fusion
  300.3 8.1 %copy.73 = bf16[3,768,768]{2,0,1:T(4,128)(2,1)} copy(bf16[3,768,768]{1,2,0:T(8,128)(2,1)} %pad_maximum_fusion) | data formatting | bytes 7077888 | tf_op jit(solution)/shard_map/stack | solution.py:169
  308.5 1.3 copy-done.12
  309.9 3.8 convolution_convert_fusion.4
  313.7 10.7 %convolution_convert_fusion.1 = bf16[768,3072]{1,0:T(8,128)(2,1)} fusion(bf16[1024,3072]{1,0:T(8,128)(2,1)} %get-tuple-element.81, f32[1024,768]{1,0:T(8,128)} %copy-done.6, f32[768]{0:T(1024)S(1)} %get-tuple-element.40, f32[768]{0:T(1024)S(1)} %get-tuple-element.41, f32[1024]{0:T(1024)S(1)} %fusion.40, f32[1024]{0:T(1024)S(1)} %broadcast_multiply_fusion.1), kind=kOutput, calls=%fused_computation.30 | convolution fusion | flops 4838129664 | bytes 14170112 | tf_op jit(solution)/shard_map/dot_general | solution.py:113
  324.5 9.3 %convolution_convert_fusion = bf16[3072,768]{1,0:T(8,128)(2,1)} fusion(bf16[1024,3072]{1,0:T(8,128)(2,1)} %get-tuple-element.59, bf16[1024,768]{1,0:T(8,128)(2,1)} %copy-done.16), kind=kOutput, calls=%fused_computation.29 | convolution fusion | flops 4834197504 | bytes 12582912 | tf_op jit(solution)/shard_map/dot_general | solution.py:109
  337.2 32.7 %all-reduce.2 = bf16[3072]{0:T(1024)(128)(2,1)S(1)} all-reduce(bf16[3072]{0:T(1024)(128)(2,1)S(1)} %get-tuple-element.80), channel_id=6, replica_groups=mesh['fsdp'=16,'rep'=2] {'fsdp'}, use_global_device_ids=true, to_apply=%region_28.29.clone | all-reduce | flops 3072 | bytes 12288
  370.1 5.1 fusion.39
  375.1 49.2 %all-reduce.8.cloned.1.call-done = bf16[3,768,768]{2,0,1:T(4,128)(2,1)} async-done(((bf16[3,768,768]{2,0,1:T(4,128)(2,1)}), bf16[3,768,768]{2,0,1:T(4,128)(2,1)}) %all-reduce.8.cloned.1.call-update) | async-done | bytes 3538960
  424.3 1.8 constant_dynamic-slice_fusion
  426.1 59.6 %reduce-scatter.7.cloned.1.call-done = bf16[48,768]{1,0:T(8,128)(2,1)} async-done(((bf16[768,768]{1,0:T(8,128)(2,1)}), bf16[48,768]{1,0:T(8,128)(2,1)}) %reduce-scatter.7.cloned.1.call-update) | async-done | bytes 73744 | tf_op jit(solution)/shard_map/reduce_scatter | solution.py:197
  485.7 78.6 %reduce-scatter.9.cloned.1.call-done = bf16[48,3072]{1,0:T(8,128)(2,1)} async-done(((bf16[768,3072]{1,0:T(8,128)(2,1)}), bf16[48,3072]{1,0:T(8,128)(2,1)}) %reduce-scatter.9.cloned.1.call-update) | async-done | bytes 294928 | tf_op jit(solution)/shard_map/reduce_scatter | solution.py:119
  564.3 78.7 %reduce-scatter.11.cloned.1.call-done = bf16[192,768]{1,0:T(8,128)(2,1)} async-done(((bf16[3072,768]{1,0:T(8,128)(2,1)}), bf16[192,768]{1,0:T(8,128)(2,1)}) %reduce-scatter.11.cloned.1.call-update) | async-done | bytes 294928 | tf_op jit(solution)/shard_map/reduce_scatter | solution.py:125
  643.0 2.9 fusion.38
  645.9 3.9 add_convert_fusion.1
  649.8 49.6 %reduce-scatter.13.cloned.1.call-done = bf16[48,8]{1,0:T(8,128)(2,1)} async-done(((bf16[768,8]{1,0:T(8,128)(2,1)}), bf16[48,8]{1,0:T(8,128)(2,1)}) %reduce-scatter.13.cloned.1.call-update) | async-done | bytes 784
  700.3 4.9 all-reduce.3
  706.3 33.3 %all-reduce.10.cloned.1.call-done = (bf16[3,48,768]{2,0,1:T(4,128)(2,1)}, bf16[48,768]{1,0:T(8,128)(2,1)}, bf16[48,3072]{1,0:T(8,128)(2,1)}, bf16[192,768]{1,0:T(8,128)(2,1)}) async-done(((bf16[3,48,768]{2,0,1:T(4,128)(2,1)}, bf16[48,768]{1,0:T(8,128)(2,1)}, bf16[48,3072]{1,0:T(8,128)(2,1)}, bf16[192,768]{1,0:T(8,128)(2,1)}), (bf16[3,48,768]{2,0,1:T(4,128)(2,1)}, bf16[48,768]{1,0:T(8,128)(2,1)}, ...) | async-done | bytes 884752 | tf_op jit(solution)/shard_map/psum | solution.py:205
  739.6 1.8 copy.74
  741.4 1.6 convert_element_type.209
  743.0 1.8 convert_element_type.215
  744.8 1.8 convert_element_type.218
  (119 shorter events, 17.8 us)
Async XLA Ops:
  7.2 62.7 %all-gather.6.cloned.1.call-start = ((), (), s32[]{:S(2)}) async-start(), calls=%async_computation.4 | async-start | bytes 3760128 | tf_op jit(solution)/shard_map/all_gather | solution.py:38
  7.9 100.6 %all-gather.8.cloned.1.call-start = ((), (), s32[]{:S(2)}) async-start(), calls=%async_computation.5 | async-start | bytes 1253376 | tf_op jit(solution)/shard_map/all_gather | solution.py:39
  8.6 146.2 %all-gather.10.cloned.1.call-start = ((), (), s32[]{:S(2)}) async-start(), calls=%async_computation.6 | async-start | bytes 5013504 | tf_op jit(solution)/shard_map/all_gather | solution.py:43
  9.4 199.3 %all-gather.12.cloned.1.call-start = ((), (), s32[]{:S(2)}) async-start(), calls=%async_computation.7 | async-start | bytes 5013504 | tf_op jit(solution)/shard_map/all_gather | solution.py:45
  10.0 414.4 %all-reduce.8.cloned.1.call-start = ((), (), s32[]{:S(2)}) async-start(), calls=%async_computation.12 | async-start | bytes 9437184
  10.7 90.7 %copy-start.21 = (pred[4,256]{1,0:T(4,128)(4,1)}, pred[4,256]{1,0:T(4,128)(4,1)S(1)}, u32[]{:S(2)}) copy-start(pred[4,256]{1,0:T(4,128)(4,1)S(1)} %broadcast_compare_fusion) | copy-start | bytes 3076
  75.0 19.5 %copy-start.4 = (bf16[4,256,12,64]{1,0,3,2:T(4,128)(2,1)}, bf16[4,256,12,64]{1,0,3,2:T(4,128)(2,1)S(1)}, u32[]{:S(2)}) copy-start(bf16[4,256,12,64]{1,0,3,2:T(4,128)(2,1)S(1)} %reshape.153) | copy-start | bytes 4718596
  83.2 11.3 %copy-start.1 = (bf16[4,256,12,64]{1,0,3,2:T(4,128)(2,1)}, bf16[4,256,12,64]{1,0,3,2:T(4,128)(2,1)S(1)}, u32[]{:S(2)}) copy-start(bf16[4,256,12,64]{1,0,3,2:T(4,128)(2,1)S(1)} %reshape.152) | copy-start | bytes 4718596
  97.6 4.8 copy-start
  97.6 4.7 copy-start.8
  112.5 96.1 %copy-start.6 = (f32[1024,768]{1,0:T(8,128)}, f32[1024,768]{1,0:T(8,128)S(1)}, u32[]{:S(2)}) copy-start(f32[1024,768]{1,0:T(8,128)S(1)} %get-tuple-element.69) | copy-start | bytes 9437188
  217.5 1.4 copy-start.3
  223.6 17.3 %copy-start.16 = (bf16[1024,768]{1,0:T(8,128)(2,1)}, bf16[1024,768]{1,0:T(8,128)(2,1)S(1)}, u32[]{:S(2)}) copy-start(bf16[1024,768]{1,0:T(8,128)(2,1)S(1)} %get-tuple-element.52) | copy-start | bytes 4718596
  223.6 17.3 %copy-start.7 = (f32[1024,768]{1,0:T(8,128)S(1)}, f32[1024,768]{1,0:T(8,128)}, u32[]{:S(2)}) copy-start(f32[1024,768]{1,0:T(8,128)} %copy-done.6) | copy-start | bytes 9437188
  252.2 1.5 copy-start.25
  252.5 1.1 copy-start.11
  256.2 6.6 copy-start.9
  256.2 6.6 copy-start.20
  256.2 6.6 copy-start.22
  271.4 8.1 %copy-start.2 = (bf16[4,256,12,64]{1,0,3,2:T(4,128)(2,1)S(1)}, bf16[4,256,12,64]{1,0,3,2:T(4,128)(2,1)}, u32[]{:S(2)}) copy-start(bf16[4,256,12,64]{1,0,3,2:T(4,128)(2,1)} %copy-done.1) | copy-start | bytes 4718596
  279.5 2.0 copy-start.5
  279.5 3.4 slice-start
  279.5 3.9 slice-start.1
  281.5 3.3 slice-start.2
  281.5 3.7 copy-start.10
  290.4 5.0 copy-start.19
  292.0 4.8 copy-start.17
  292.1 2.0 copy-start.24
  293.7 1.8 copy-start.13
  308.4 1.4 copy-start.12
  308.5 177.2 %reduce-scatter.7.cloned.1.call-start = ((), (), s32[]{:S(2)}) async-start(), calls=%async_computation.8 | async-start | bytes 1253376 | tf_op jit(solution)/shard_map/reduce_scatter | solution.py:197
  313.7 250.6 %reduce-scatter.9.cloned.1.call-start = ((), (), s32[]{:S(2)}) async-start(), calls=%async_computation.9 | async-start | bytes 5013504 | tf_op jit(solution)/shard_map/reduce_scatter | solution.py:119
  324.4 318.5 %reduce-scatter.11.cloned.1.call-start = ((), (), s32[]{:S(2)}) async-start(), calls=%async_computation.10 | async-start | bytes 5013504 | tf_op jit(solution)/shard_map/reduce_scatter | solution.py:125
  333.8 0.7 copy-start.23
  333.8 365.7 %reduce-scatter.13.cloned.1.call-start = ((), (), s32[]{:S(2)}) async-start(), calls=%async_computation.11 | async-start | bytes 208896
  369.9 369.7 %all-reduce.10.cloned.1.call-start = ((), (), s32[]{:S(2)}) async-start(), calls=%async_computation.13 | async-start | bytes 1916928 | tf_op jit(solution)/shard_map/psum | solution.py:205
  370.1 272.9 %copy-start.18 = (bf16[96,8,4,256]{3,1,2,0:T(8,128)(2,1)S(1)}, bf16[96,8,4,256]{3,1,2,0:T(8,128)(2,1)}, u32[]{:S(2)}) copy-start(bf16[96,8,4,256]{3,1,2,0:T(8,128)(2,1)} %copy-done.17) | copy-start | bytes 4718596
  643.0 2.9 copy-start.14
  643.0 2.9 copy-start.15
Sparse Core Ops, SparseCore 0:
  10.3 50.7 all-gather.5
  63.3 37.0 all-gather.7
  102.8 51.9 all-gather.9
  156.9 51.6 all-gather.11
  308.6 115.6 all-reduce.7
  427.8 57.8 reduce-scatter.6
  489.6 74.6 reduce-scatter.8
  568.2 74.7 reduce-scatter.10
  647.0 52.4 reduce-scatter.12
  702.4 37.1 all-reduce.9
where the time goes:
time: 765 us; the launch traced here: 754 us
  waiting for transfers between devices  410 us (54%)
  matrix products  152 us (20%)
  blocking collectives  92.3 us (12%)
  local copies, waits for them, and re-layouts  50.5 us (7%)
  other arithmetic  31.3 us (4%)
  between operations  17.2 us (2%)
    unnamed x12, waiting for transfers between devices  102 us
    reduce_scatter x1, waiting for transfers between devices, body(): lax.psum_scatter(grad_down.astype(jnp.bfloat16), 'fsdp', scatter_dimensio...  78.7 us
    reduce_scatter x1, waiting for transfers between devices, body(): lax.psum_scatter(grad_up.astype(jnp.bfloat16), 'fsdp', scatter_dimension=...  78.6 us
    unnamed x2, blocking collectives  64 us
    reduce_scatter x1, waiting for transfers between devices, body(): lax.psum_scatter(grad_out.astype(jnp.bfloat16), 'fsdp', scatter_dimension...  59.6 us
    all_gather x1, waiting for transfers between devices, body(): lax.all_gather(up_weight, 'fsdp', axis=0, tiled=True)  40.7 us
    dot_general x1, matrix products, body(): jnp.dot(normed_low, in_all, preferred_element_type=jnp.float32)  36.1 us
    psum x1, waiting for transfers between devices, body(): lax.psum(attn_parts[0].astype(jnp.bfloat16), 'rep').astype(jnp.float32)  33.3 us
  transfers between devices with their start and end apart: 10, of which 8 were waited for; matrix products, arithmetic and copies ran while one was open for 17% of the time, Pallas kernels for 0%

commit v1 on v0

--- a/solution.py
+++ b/solution.py
@@ -202,7 +202,9 @@
         ).astype(jnp.float32),
     )
     attn_parts = (
-        lax.psum(attn_parts[0].astype(jnp.bfloat16), "rep").astype(jnp.float32),
+        jnp.sum(lax.all_gather(attn_parts[0].astype(jnp.bfloat16), "rep"), axis=0).astype(
+            jnp.float32
+        ),
         lax.psum(attn_parts[1].astype(jnp.bfloat16), "rep").astype(jnp.float32),
         lax.psum(attn_parts[2].astype(jnp.bfloat16), "rep").astype(jnp.float32),
     )

time: 765 us -> 704 us (0.920)
  waiting for transfers between devices: 410 us -> 345 us
  local copies, waits for them, and re-layouts: 50.5 us -> 42.8 us
    unnamed x12, waiting for transfers between devices: 102 us -> 166 us
    reduce_scatter x1, waiting for transfers between devices: 78.6 us -> 16.9 us  [body(): lax.psum_scatter(grad_up.astype(jnp.bfloat16), 'fsdp', scatter_dimension=...]
    reduce_scatter x1, waiting for transfers between devices: 59.6 us -> 0.01 us  [body(): lax.psum_scatter(grad_out.astype(jnp.bfloat16), 'fsdp', scatter_dimension...]
    psum x1, waiting for transfers between devices: 33.3 us -> 24.4 us  [body(): lax.psum(attn_parts[1].astype(jnp.bfloat16), 'rep').astype(jnp.float32)]
    unnamed x71 -> x76, local copies, waits for them, and re-layouts: 17.6 us -> 14 us
  transfers between devices with their start and end apart: 10 -> 10, of which waited for: 8 -> 7; matrix products, arithmetic and copies ran while one was open for 17% -> 25% of each run, Pallas kernels for 0% -> 0%
where the time goes in v1:
time: 704 us; the launch traced here: 693 us
  waiting for transfers between devices  345 us (49%)
  matrix products  157 us (22%)
  blocking collectives  99.1 us (14%)
  local copies, waits for them, and re-layouts  42.8 us (6%)
  other arithmetic  30.7 us (4%)
  between operations  17.3 us (2%)
    unnamed x12, waiting for transfers between devices  166 us
    reduce_scatter x1, waiting for transfers between devices, body(): lax.psum_scatter(grad_down.astype(jnp.bfloat16), 'fsdp', scatter_dimensio...  78.7 us
    unnamed x2, blocking collectives  63.8 us
    all_gather x1, waiting for transfers between devices, body(): lax.all_gather(up_weight, 'fsdp', axis=0, tiled=True)  41.7 us
    dot_general x1, matrix products, body(): jnp.dot(normed_low, in_all, preferred_element_type=jnp.float32)  36.1 us
    psum x1, waiting for transfers between devices, body(): lax.psum(attn_parts[1].astype(jnp.bfloat16), 'rep').astype(jnp.float32)  24.4 us
    all_gather x1, blocking collectives, body(): lax.all_gather(vectors, 'fsdp', axis=1, tiled=True)  23.5 us
    all_gather x1, waiting for transfers between devices, body(): lax.all_gather(down_weight, 'fsdp', axis=0, tiled=True)  17.7 us
  transfers between devices with their start and end apart: 10, of which 7 were waited for; matrix products, arithmetic and copies ran while one was open for 25% of the time, Pallas kernels for 0%

profile of v1, /device:TPU:0, one launch (start us, length us, event | category | flops | bytes accessed | tf_op | source)
XLA Modules:
  0.0 693.1 jit_solution(5215666654349846593)
XLA Ops:
  10.7 1.3 fusion.54
  12.0 23.5 %all-gather.1 = bf16[16,48,8]{1,2,0:T(8,128)(2,1)S(1)} all-gather(bf16[1,48,8]{1,2,0:T(8,128)(2,1)} %bitcast.140), channel_id=1, replica_groups=mesh['fsdp'=16,'rep'=2] {'fsdp'}, dimensions={0}, use_global_device_ids=true | all-gather | bytes 13056 | tf_op jit(solution)/shard_map/all_gather | solution.py:40
  35.6 1.3 fusion.55
  38.5 31.3 %all-reduce = bf16[3072]{0:T(1024)(128)(2,1)S(1)} all-reduce(bf16[3072]{0:T(1024)(128)(2,1)S(1)} %dynamic-update-slice), channel_id=1, replica_groups=mesh['fsdp'=16,'rep'=2] {'fsdp'}, use_global_device_ids=true, to_apply=%add | all-reduce | flops 3072 | bytes 12288
  69.8 3.2 convolution_convert_fusion.3
  73.8 1.2 reshape.153
  75.0 3.7 add_convert_fusion.4
  78.7 1.6 copy.52
  80.3 2.9 reshape.152
  83.2 4.8 add_convert_fusion.5
  88.1 2.6 copy.51
  90.6 3.9 reshape.151
  94.5 3.1 fusion.12
  97.6 3.9 fusion.6
  102.4 3.4 fusion.22
  105.8 1.2 copy.58
  107.0 1.5 copy.82
  108.5 4.0 fusion.56
  113.1 41.7 %all-gather.11.cloned.1.call-done = bf16[768,3072]{1,0:T(8,128)(2,1)} async-done(((bf16[48,3072]{1,0:T(8,128)(2,1)}), bf16[768,3072]{1,0:T(8,128)(2,1)}) %all-gather.11.cloned.1.call-update) | async-done | bytes 4718608 | tf_op jit(solution)/shard_map/all_gather | solution.py:43
  154.8 36.1 %multiply_convert_fusion.1 = (bf16[1024,3072]{1,0:T(8,128)(2,1)}, f32[1024,3072]{1,0:T(8,128)}, f32[1024,3072]{1,0:T(8,128)}) fusion(f32[3072]{0:T(1024)S(1)} %convert_element_type.184, bf16[768,3072]{1,0:T(8,128)(2,1)} %all-gather.11.cloned.1.call-done, f32[1024,768]{1,0:T(8,128)S(1)} %get-tuple-element.52, f32[768]{0:T(1024)S(1)} %get-tuple-element.24, ...), kind=kOutput, calls=%fused_computation.6 | convolution fusion | flops 5043388416 | bytes 39348224 | tf_op jit(solution)/shard_map/dot_general | solution.py:91
  190.9 17.7 %all-gather.13.cloned.1.call-done = bf16[3072,768]{1,0:T(8,128)(2,1)} async-done(((bf16[192,768]{1,0:T(8,128)(2,1)}), bf16[3072,768]{1,0:T(8,128)(2,1)}) %all-gather.13.cloned.1.call-update) | async-done | bytes 4718608 | tf_op jit(solution)/shard_map/all_gather | solution.py:45
  208.6 8.8 %fusion.57 = (f32[1024]{0:T(1024)S(1)}, f32[1024,768]{1,0:T(8,128)S(1)}) fusion(f32[768]{0:T(1024)S(1)} %get-tuple-element.23, bf16[1024,3072]{1,0:T(8,128)(2,1)} %get-tuple-element.42, bf16[3072,768]{1,0:T(8,128)(2,1)} %all-gather.13.cloned.1.call-done, f32[768]{0:T(1024)S(1)} %get-tuple-element.24, f32[768]{0:T(1024)S(1)} %get-tuple-element.25, ...), kind=kOutput, calls=%fused_computation.120 | convolution fusion | flops 4837342208 | bytes 17323008 | tf_op jit(solution)/shard_map/dot_general | solution.py:97
  218.9 1.5 multiply_reduce_fusion.2
  220.4 2.8 fusion.52
  223.6 17.3 %fusion.60 = (bf16[3072]{0:T(1024)(128)(2,1)S(1)}, bf16[1024,3072]{1,0:T(8,128)(2,1)}) fusion(f32[1024,3072]{1,0:T(8,128)} %get-tuple-element.43, bf16[1024,768]{1,0:T(8,128)(2,1)S(1)} %get-tuple-element.35, bf16[3072,768]{1,0:T(8,128)(2,1)} %all-gather.13.cloned.1.call-done, f32[1024,3072]{1,0:T(8,128)} %get-tuple-element.53, ...), kind=kOutput, calls=%fused_computation.123 | convolution fusion | flops 4882166784 | bytes 37767168 | tf_op jit(solution)/shard_map/dot_general | solution.py:111
  241.0 9.7 %multiply_reduce_fusion.3 = (bf16[768]{0:T(1024)(128)(2,1)S(1)}, f32[1024]{0:T(1024)S(1)}, bf16[768]{0:T(1024)(128)(2,1)S(1)}, f32[1024,768]{1,0:T(8,128)S(1)}) fusion(f32[1024,768]{1,0:T(8,128)S(1)} %copy-done.7, f32[1024]{0:T(1024)S(1)} %fusion.40, f32[1024]{0:T(1024)S(1)} %broadcast_multiply_fusion.1, f32[768]{0:T(1024)S(1)} %get-tuple-element.25, ...), kind=kOutput, calls=%fused_computation.37 | convolution fusion | flops 4839699456 | bytes 18892800 | tf_op jit(solution)/shard_map/dot_general | solution.py:115
  250.7 1.5 fusion.51
  252.5 1.2 copy-done.17
  253.8 2.4 convolution_convert_fusion.4
  256.3 10.4 %convolution_convert_fusion.1 = bf16[768,3072]{1,0:T(8,128)(2,1)} fusion(bf16[1024,3072]{1,0:T(8,128)(2,1)} %get-tuple-element.64, f32[1024,768]{1,0:T(8,128)} %copy-done.6, f32[768]{0:T(1024)S(1)} %get-tuple-element.24, f32[768]{0:T(1024)S(1)} %get-tuple-element.25, f32[1024]{0:T(1024)S(1)} %fusion.40, f32[1024]{0:T(1024)S(1)} %broadcast_multiply_fusion.1), kind=kOutput, calls=%fused_computation.30 | convolution fusion | flops 4838129664 | bytes 14170112 | tf_op jit(solution)/shard_map/dot_general | solution.py:113
  266.7 9.3 %convolution_convert_fusion = bf16[3072,768]{1,0:T(8,128)(2,1)} fusion(bf16[1024,3072]{1,0:T(8,128)(2,1)} %get-tuple-element.42, bf16[1024,768]{1,0:T(8,128)(2,1)} %copy-done.14), kind=kOutput, calls=%fused_computation.29 | convolution fusion | flops 4834197504 | bytes 12582912 | tf_op jit(solution)/shard_map/dot_general | solution.py:109
  277.2 2.7 convolution_convert_fusion.2
  279.9 1.9 copy.59
  281.7 2.9 reshape.155
  284.7 7.8 %multiply_reduce_fusion = (f32[4,12,256]{2,1,0:T(8,128)S(1)}, f32[4,12,256,256]{2,3,1,0:T(8,128)S(1)}) fusion(f32[4,12,256]{2,1,0:T(8,128)S(1)} %log_add_fusion, f32[4,12,256,256]{2,3,1,0:T(8,128)} %copy-done, pred[4,256]{1,0:T(4,128)(4,1)S(1)} %copy-done.25, bf16[4,256,12,64]{1,0,3,2:T(4,128)(2,1)S(1)} %copy-done.9, bf16[4,256,12,64]{1,0,3,2:T(4,128)(2,1)S(1)} %reshape.155), kind=kOutput, calls=%fused_computation.3 | convolution fusion | flops 418369536 | bytes 28410880 | tf_op jit(solution)/shard_map/nqhe,nkhe->nhqk/dot_general | solution.py:153
  292.5 8.0 %multiply_convert_fusion = bf16[4,12,256,256]{2,3,1,0:T(8,128)(2,1)S(1)} fusion(f32[4,12,256,256]{2,3,1,0:T(8,128)S(1)} %get-tuple-element.58, f32[4,12,256]{2,1,0:T(8,128)S(1)} %get-tuple-element.57, f32[4,12,256]{2,1,0:T(8,128)S(1)} %log_add_fusion, f32[4,12,256,256]{2,3,1,0:T(8,128)} %copy-done, pred[4,256]{1,0:T(4,128)(4,1)S(1)} %copy-done.25), kind=kLoop, calls=%fused_computation.2 | loop fusion | flops 18874368 | bytes 31556608 | tf_op jit(solution)/shard_map/convert_element_type | solution.py:158
  300.6 2.0 fusion.24
  302.6 1.2 copy.67
  304.4 1.3 fusion.58
  305.7 1.2 copy.64
  307.0 1.6 copy.84
  308.5 3.7 fusion.59
  312.2 1.2 copy.70
  315.0 4.0 fusion.27
  319.0 2.4 fusion.26
  321.4 2.4 fusion.25
  323.9 2.4 pad_maximum_fusion
  326.3 5.7 copy.71
  333.5 32.5 %all-reduce.2 = bf16[3072]{0:T(1024)(128)(2,1)S(1)} all-reduce(bf16[3072]{0:T(1024)(128)(2,1)S(1)} %get-tuple-element.63), channel_id=7, replica_groups=mesh['fsdp'=16,'rep'=2] {'fsdp'}, use_global_device_ids=true, to_apply=%region_28.29.clone | all-reduce | flops 3072 | bytes 12288
  366.1 4.5 fusion.39
  370.6 4.6 fusion.38
  375.1 16.9 %reduce-scatter.9.cloned.1.call-done = bf16[48,3072]{1,0:T(8,128)(2,1)} async-done(((bf16[768,3072]{1,0:T(8,128)(2,1)}), bf16[48,3072]{1,0:T(8,128)(2,1)}) %reduce-scatter.9.cloned.1.call-update) | async-done | bytes 294928 | tf_op jit(solution)/shard_map/reduce_scatter | solution.py:119
  392.0 78.7 %reduce-scatter.11.cloned.1.call-done = bf16[192,768]{1,0:T(8,128)(2,1)} async-done(((bf16[3072,768]{1,0:T(8,128)(2,1)}), bf16[192,768]{1,0:T(8,128)(2,1)}) %reduce-scatter.11.cloned.1.call-update) | async-done | bytes 294928 | tf_op jit(solution)/shard_map/reduce_scatter | solution.py:125
  470.8 5.9 add_convert_fusion.1
  476.6 50.6 %reduce-scatter.13.cloned.1.call-done = bf16[48,8]{1,0:T(8,128)(2,1)} async-done(((bf16[768,8]{1,0:T(8,128)(2,1)}), bf16[48,8]{1,0:T(8,128)(2,1)}) %reduce-scatter.13.cloned.1.call-update) | async-done | bytes 784
  528.0 4.9 all-reduce.3
  534.1 112.7 %all-reduce.8.cloned.1.call-done = bf16[3,768,768]{2,0,1:T(4,128)(2,1)} async-done(((bf16[3,768,768]{2,0,1:T(4,128)(2,1)}), bf16[3,768,768]{2,0,1:T(4,128)(2,1)}) %all-reduce.8.cloned.1.call-update) | async-done | bytes 3538960
  646.8 1.1 constant_dynamic-slice_fusion
  647.9 6.9 all-gather
  655.2 1.0 copy.74
  656.2 24.4 %all-reduce.10.cloned.1.call-done = (bf16[48,768]{1,0:T(8,128)(2,1)}, bf16[48,3072]{1,0:T(8,128)(2,1)}, bf16[192,768]{1,0:T(8,128)(2,1)}) async-done(((bf16[48,768]{1,0:T(8,128)(2,1)}, bf16[48,3072]{1,0:T(8,128)(2,1)}, bf16[192,768]{1,0:T(8,128)(2,1)}), (bf16[48,768]{1,0:T(8,128)(2,1)}, bf16[48,3072]{1,0:T(8,128)(2,1)}, bf16[192,768]{1,0:T(8,128)(2,1)})) %all-reduce.10.cloned.1.call-update) | async-done | bytes 663568 | tf_op jit(solution)/shard_map/psum | solution.py:208
  680.6 1.6 convert_element_type.211
  682.2 1.8 convert_element_type.217
  684.0 1.8 convert_element_type.220
  (127 shorter events, 14.7 us)
Async XLA Ops:
  7.2 62.7 %all-gather.7.cloned.1.call-start = ((), (), s32[]{:S(2)}) async-start(), calls=%async_computation.4 | async-start | bytes 3760128 | tf_op jit(solution)/shard_map/all_gather | solution.py:38
  7.9 100.6 %all-gather.9.cloned.1.call-start = ((), (), s32[]{:S(2)}) async-start(), calls=%async_computation.5 | async-start | bytes 1253376 | tf_op jit(solution)/shard_map/all_gather | solution.py:39
  8.6 146.1 %all-gather.11.cloned.1.call-start = ((), (), s32[]{:S(2)}) async-start(), calls=%async_computation.6 | async-start | bytes 5013504 | tf_op jit(solution)/shard_map/all_gather | solution.py:43
  9.4 199.3 %all-gather.13.cloned.1.call-start = ((), (), s32[]{:S(2)}) async-start(), calls=%async_computation.7 | async-start | bytes 5013504 | tf_op jit(solution)/shard_map/all_gather | solution.py:45
  10.0 365.2 %reduce-scatter.7.cloned.1.call-start = ((), (), s32[]{:S(2)}) async-start(), calls=%async_computation.8 | async-start | bytes 1253376 | tf_op jit(solution)/shard_map/reduce_scatter | solution.py:197
  10.7 90.8 %copy-start.24 = (pred[4,256]{1,0:T(4,128)(4,1)}, pred[4,256]{1,0:T(4,128)(4,1)S(1)}, u32[]{:S(2)}) copy-start(pred[4,256]{1,0:T(4,128)(4,1)S(1)} %broadcast_compare_fusion) | copy-start | bytes 3076
  75.0 19.5 %copy-start.4 = (bf16[4,256,12,64]{1,0,3,2:T(4,128)(2,1)}, bf16[4,256,12,64]{1,0,3,2:T(4,128)(2,1)S(1)}, u32[]{:S(2)}) copy-start(bf16[4,256,12,64]{1,0,3,2:T(4,128)(2,1)S(1)} %reshape.153) | copy-start | bytes 4718596
  83.2 11.3 %copy-start.1 = (bf16[4,256,12,64]{1,0,3,2:T(4,128)(2,1)}, bf16[4,256,12,64]{1,0,3,2:T(4,128)(2,1)S(1)}, u32[]{:S(2)}) copy-start(bf16[4,256,12,64]{1,0,3,2:T(4,128)(2,1)S(1)} %reshape.152) | copy-start | bytes 4718596
  97.6 4.8 copy-start
  97.6 4.8 copy-start.20
  97.6 4.8 copy-start.8
  102.4 3.4 copy-start.22
  112.6 96.1 %copy-start.6 = (f32[1024,768]{1,0:T(8,128)}, f32[1024,768]{1,0:T(8,128)S(1)}, u32[]{:S(2)}) copy-start(f32[1024,768]{1,0:T(8,128)S(1)} %get-tuple-element.52) | copy-start | bytes 9437188
  217.5 1.4 copy-start.3
  223.6 17.3 %copy-start.14 = (bf16[1024,768]{1,0:T(8,128)(2,1)}, bf16[1024,768]{1,0:T(8,128)(2,1)S(1)}, u32[]{:S(2)}) copy-start(bf16[1024,768]{1,0:T(8,128)(2,1)S(1)} %get-tuple-element.35) | copy-start | bytes 4718596
  223.6 17.3 %copy-start.7 = (f32[1024,768]{1,0:T(8,128)S(1)}, f32[1024,768]{1,0:T(8,128)}, u32[]{:S(2)}) copy-start(f32[1024,768]{1,0:T(8,128)} %copy-done.6) | copy-start | bytes 9437188
  252.2 1.6 copy-start.17
  252.5 24.6 %copy-start.10 = (bf16[1024,768]{1,0:T(8,128)(2,1)}, bf16[1024,768]{1,0:T(8,128)(2,1)S(1)}, u32[]{:S(2)}) copy-start(bf16[1024,768]{1,0:T(8,128)(2,1)S(1)} %get-tuple-element.37) | copy-start | bytes 4718596
  256.2 135.8 %reduce-scatter.9.cloned.1.call-start = ((), (), s32[]{:S(2)}) async-start(), calls=%async_computation.9 | async-start | bytes 5013504 | tf_op jit(solution)/shard_map/reduce_scatter | solution.py:119
  266.7 204.0 %reduce-scatter.11.cloned.1.call-start = ((), (), s32[]{:S(2)}) async-start(), calls=%async_computation.10 | async-start | bytes 5013504 | tf_op jit(solution)/shard_map/reduce_scatter | solution.py:125
  276.0 0.7 copy-start.26
  276.0 1.1 copy-start.21
  276.0 1.1 copy-start.23
  276.0 251.2 %reduce-scatter.13.cloned.1.call-start = ((), (), s32[]{:S(2)}) async-start(), calls=%async_computation.11 | async-start | bytes 208896
  279.8 4.8 copy-start.9
  279.9 4.8 copy-start.25
  292.5 8.1 %copy-start.2 = (bf16[4,256,12,64]{1,0,3,2:T(4,128)(2,1)S(1)}, bf16[4,256,12,64]{1,0,3,2:T(4,128)(2,1)}, u32[]{:S(2)}) copy-start(bf16[4,256,12,64]{1,0,3,2:T(4,128)(2,1)} %copy-done.1) | copy-start | bytes 4718596
  300.6 8.0 %slice-start = ((s8[12582912]{0:T(1024)(128)(4,1)}), s8[4194304]{0:T(1024)(128)(4,1)S(1)}, s32[]{:S(2)}) async-start(s8[12582912]{0:T(1024)(128)(4,1)} %bitcast.118), calls=%async_computation.14 | async-start | bytes 8388608
  300.6 8.0 %slice-start.1 = ((s8[12582912]{0:T(1024)(128)(4,1)}), s8[4194304]{0:T(1024)(128)(4,1)S(1)}, s32[]{:S(2)}) async-start(s8[12582912]{0:T(1024)(128)(4,1)} %bitcast.118), calls=%async_computation.15 | async-start | bytes 8388608
  302.6 1.8 copy-start.5
  304.4 14.6 %copy-start.15 = (bf16[96,8,4,256]{3,1,2,0:T(8,128)(2,1)}, bf16[96,8,4,256]{3,1,2,0:T(8,128)(2,1)S(1)}, u32[]{:S(2)}) copy-start(bf16[96,8,4,256]{3,1,2,0:T(8,128)(2,1)S(1)} %copy.85) | copy-start | bytes 4718596
  304.4 4.1 slice-start.2
  313.8 5.2 copy-start.12
  315.0 4.0 copy-start.27
  319.0 2.4 copy-start.18
  323.9 322.9 %all-reduce.8.cloned.1.call-start = ((), (), s32[]{:S(2)}) async-start(), calls=%async_computation.12 | async-start | bytes 9437184
  332.0 34.1 %copy-start.16 = (bf16[96,8,4,256]{3,1,2,0:T(8,128)(2,1)S(1)}, bf16[96,8,4,256]{3,1,2,0:T(8,128)(2,1)}, u32[]{:S(2)}) copy-start(bf16[96,8,4,256]{3,1,2,0:T(8,128)(2,1)} %copy-done.15) | copy-start | bytes 4718596
  332.0 348.6 %all-reduce.10.cloned.1.call-start = ((), (), s32[]{:S(2)}) async-start(), calls=%async_computation.13 | async-start | bytes 1327104 | tf_op jit(solution)/shard_map/psum | solution.py:208
  366.1 4.5 copy-start.19
  370.6 100.2 %copy-start.11 = (bf16[1024,768]{1,0:T(8,128)(2,1)S(1)}, bf16[1024,768]{1,0:T(8,128)(2,1)}, u32[]{:S(2)}) copy-start(bf16[1024,768]{1,0:T(8,128)(2,1)} %copy-done.10) | copy-start | bytes 4718596
  370.6 100.2 %copy-start.13 = (bf16[96,8,4,256]{3,1,2,0:T(8,128)(2,1)S(1)}, bf16[96,8,4,256]{3,1,2,0:T(8,128)(2,1)}, u32[]{:S(2)}) copy-start(bf16[96,8,4,256]{3,1,2,0:T(8,128)(2,1)} %copy-done.12) | copy-start | bytes 4718596
Sparse Core Ops, SparseCore 0:
  10.3 50.7 all-gather.6
  63.3 37.0 all-gather.8
  102.8 51.9 all-gather.10
  156.9 51.6 all-gather.12
  256.3 56.7 reduce-scatter.6
  316.9 75.1 reduce-scatter.8
  395.9 74.7 reduce-scatter.10
  474.8 52.3 reduce-scatter.12
  530.9 115.8 all-reduce.7
  649.1 31.5 all-reduce.9
